TPU v7x, 32 devices: a whole 2x2x4 slice. The times are simulated.
32 devices in a mesh: space: 8 (over z, core), tm: 4 (over y, x).
Axes of the slice: x: 2, y: 2, z: 4, core: 2. Of those that a mesh axis runs over, the one named last changes fastest.
Arguments:
- snapshots: bfloat16 [32768, 512], P('space', 'tm'), may hold values from -6 to 6
- stencil_starts: int32 [512], P('tm'), may hold values from 0 to 508, as said below
- stencil_widths: int32 [512], P('tm'), may hold values from 4 to 40, as said below
- stencil_coeffs: bfloat16 [512, 40], P('tm'), may hold values from -2 to 2
- panels: bfloat16 [512, 256], P('tm'), may hold values from -0.25 to 0.25
Outputs:
- gram: float32 [512, 512], P(('tm', 'space'))
- modes: bfloat16 [32768, 256], P(('space', 'tm'))
Inputs may be any that keep to these rules, and one draw needn't show every extreme that they name: `stencil_starts`: uniform time u's stencil starts inside its own time block, snapshots from (u // 128) * 128 to that plus 128 - 1, and ends before snapshot 512. `stencil_widths`: some stencil has width 40 and some has width 4.
All inputs are finite; a program needn't handle non-finite values.
Results may differ from a plain program's by a relative error of at most 0.0049.
Values may be sent and summed in bfloat16 or wider, within the bound.
A program may use at most 64 MiB of HBM per device.

v0:
```python
import jax
import jax.numpy as jnp
from jax import lax
from jax.sharding import PartitionSpec as P


def shifted(value, axis, steps):
    count = lax.axis_size(axis)
    initial, last = (max(0, -steps), min(count, count - steps))
    return lax.ppermute(value, axis, [(source, source + steps) for source in range(initial, last)])


def on_device(snapshots, stencil_starts, stencil_widths, stencil_coeffs, panels):
    rows, block = snapshots.shape
    width_max = stencil_coeffs.shape[1]
    rim = shifted(snapshots[:, : width_max - 1], "tm", -1)
    extended = jnp.concatenate([snapshots, rim], axis=1)
    offsets = stencil_starts - lax.axis_index("tm") * block
    position = jnp.arange(block + width_max - 1, dtype=jnp.int32)[:, None]
    relative = position - offsets[None, :]
    steps = jnp.arange(width_max, dtype=jnp.int32)[:, None, None]
    picked = (relative[None, :, :] == steps) & (steps < stencil_widths[None, None, :])
    coeff_table = stencil_coeffs.T[:, None, :].astype(jnp.float32)
    weights = jnp.sum(jnp.where(picked, coeff_table, 0.0), axis=0).astype(jnp.bfloat16)
    resampled = jnp.dot(extended, weights, preferred_element_type=jnp.float32).astype(jnp.bfloat16)
    scale = 1.0 / (rows * lax.axis_size("space"))
    share = rows // lax.axis_size("tm")
    whole = lax.all_gather(resampled, "tm", axis=1, tiled=True)
    partial_value = lax.dot_general(
        resampled, whole, (((0,), (0,)), ((), ())), preferred_element_type=jnp.float32
    )
    every_panel = lax.all_gather(panels, "tm", axis=0, tiled=True)
    mine = lax.dynamic_slice_in_dim(whole, lax.axis_index("tm") * share, share, 0)
    modes = jnp.dot(mine, every_panel, preferred_element_type=jnp.float32).astype(jnp.bfloat16)
    partial_value = partial_value * scale
    gram = lax.psum_scatter(partial_value, "space", scatter_dimension=0, tiled=True)
    return (gram, modes)


def solution(mesh):
    return jax.shard_map(
        on_device,
        mesh=mesh,
        in_specs=(P("space", "tm"), P("tm"), P("tm"), P("tm", None), P("tm", None)),
        out_specs=(P(("tm", "space"), None), P(("space", "tm"), None)),
        check_vma=False,
    )
```

profile of v0, /device:TPU:0, one launch (start us, length us, event | category | flops | bytes accessed | tf_op | source)
XLA Modules:
  0.0 120.7 jit_solution(11758978963417569077)
XLA Ops:
  7.2 0.0 all-gather.2.cloned.1.call-start
  7.2 1.6 %copy.11 = bf16[4096,39]{0,1:T(8,128)(2,1)S(1)} copy(bf16[4096,39]{1,0:T(8,128)(2,1)} %bitcast.7) | data formatting | bytes 638976
  8.8 1.3 %collective-permute-start = (bf16[4096,39]{0,1:T(8,128)(2,1)S(1)}, bf16[4096,39]{0,1:T(8,128)(2,1)S(1)}, u32[]{:S(2)}, u32[]{:S(2)}) collective-permute-start(bf16[4096,39]{0,1:T(8,128)(2,1)S(1)} %copy.11), channel_id=1, source_target_pairs={{1,0},{2,1},{3,2},{5,4},{6,5},{7,6},{9,8},{10,9},{11,10},{13,12},{... | collective-permute-start | bytes 958472 | tf_op jit(solution)/shard_map/ppermute | solution.py:10
  10.1 0.7 convert_bitcast_fusion
  10.8 0.7 broadcast_subtract_fusion
  11.5 0.7 iota_compare_fusion.1
  12.2 1.4 %select_reduce_fusion = bf16[167,128]{1,0:T(8,128)(2,1)S(1)} fusion(f32[40,128]{1,0:T(8,128)S(1)} %convert_bitcast_fusion, s32[167,128]{1,0:T(8,128)S(1)} %iota_subtract_fusion, pred[40,128]{1,0:T(8,128)(4,1)S(1)} %iota_compare_fusion.1), kind=kLoop, calls=%fused_computation.1 | loop fusion | flops 3398784 | bytes 153856 | tf_op jit(solution)/shard_map/reduce_sum | solution.py:24
  13.6 7.8 %collective-permute-done = bf16[4096,39]{0,1:T(8,128)(2,1)S(1)} collective-permute-done((bf16[4096,39]{0,1:T(8,128)(2,1)S(1)}, bf16[4096,39]{0,1:T(8,128)(2,1)S(1)}, u32[]{:S(2)}, u32[]{:S(2)}) %collective-permute-start) | collective-permute-done | bytes 319520 | tf_op jit(solution)/shard_map/ppermute | solution.py:10
  21.4 0.5 copy.10
  21.9 2.9 %convolution_convert_fusion = bf16[4096,128]{1,0:T(8,128)(2,1)} fusion(bf16[4096,39]{1,0:T(8,128)(2,1)S(1)} %copy.10, bf16[4096,128]{1,0:T(8,128)(2,1)} %param.5, bf16[167,128]{1,0:T(8,128)(2,1)S(1)} %select_reduce_fusion), kind=kOutput, calls=%fused_computation | convolution fusion | flops 178372608 | bytes 2459392 | tf_op jit(solution)/shard_map/dot_general | solution.py:25
  24.8 0.0 copy-start
  24.8 0.0 all-gather.2.cloned.1.call-update
  24.8 0.0 reduce-scatter.2.cloned.1.call-start
  24.9 54.0 %all-gather.2.cloned.1.call-done = bf16[4096,512]{1,0:T(8,128)(2,1)} async-done(((bf16[4096,128]{1,0:T(8,128)(2,1)}), bf16[4096,512]{1,0:T(8,128)(2,1)}) %all-gather.2.cloned.1.call-update) | async-done | bytes 4194320 | tf_op jit(solution)/shard_map/all_gather | solution.py:28
  78.9 4.0 %convolution_multiply_fusion = f32[128,512]{1,0:T(8,128)} fusion(bf16[4096,128]{1,0:T(8,128)(2,1)} %convolution_convert_fusion, bf16[4096,512]{1,0:T(8,128)(2,1)} %all-gather.2.cloned.1.call-done), kind=kOutput, calls=%fused_computation.8 | convolution fusion | flops 536936448 | bytes 5505024 | tf_op jit(solution)/shard_map/dot_general | solution.py:29
  82.8 0.0 reduce-scatter.2.cloned.1.call-update
  82.9 0.0 copy-done
  82.9 9.0 %all_gather.7 = bf16[512,256]{1,0:T(8,128)(2,1)S(1)} all-gather(bf16[128,256]{1,0:T(8,128)(2,1)S(1)} %copy-done), channel_id=1, replica_groups=mesh['space'=8,'tm'=4] {'tm'}, dimensions={0}, use_global_device_ids=true | all-gather | bytes 327680 | tf_op jit(solution)/shard_map/all_gather | solution.py:32
  91.9 2.5 %convolution_convert_fusion.1 = bf16[1024,256]{1,0:T(8,128)(2,1)} fusion(bf16[512,256]{1,0:T(8,128)(2,1)S(1)} %all_gather.7, bf16[4096,512]{1,0:T(8,128)(2,1)} %all-gather.2.cloned.1.call-done, s32[]{:T(128)S(6)} %select_n.8), kind=kOutput, calls=%fused_computation.7 | convolution fusion | flops 268697600 | bytes 1835012 | tf_op jit(solution)/shard_map/dot_general | solution.py:34
  94.3 19.6 %reduce-scatter.2.cloned.1.call-done = f32[16,512]{1,0:T(8,128)} async-done(((f32[128,512]{1,0:T(8,128)}), f32[16,512]{1,0:T(8,128)}) %reduce-scatter.2.cloned.1.call-update) | async-done | bytes 32784 | tf_op jit(solution)/shard_map/reduce_scatter | solution.py:36
  (1 shorter events, 0.0 us)
Async XLA Ops:
  7.2 71.7 %all-gather.2.cloned.1.call-start = ((), (), s32[]{:S(2)}) async-start(), calls=%async_computation.1 | async-start | bytes 5242880 | tf_op jit(solution)/shard_map/all_gather | solution.py:28
  8.8 12.6 %collective-permute-start = (bf16[4096,39]{0,1:T(8,128)(2,1)S(1)}, bf16[4096,39]{0,1:T(8,128)(2,1)S(1)}, u32[]{:S(2)}, u32[]{:S(2)}) collective-permute-start(bf16[4096,39]{0,1:T(8,128)(2,1)S(1)} %copy.11), channel_id=1, source_target_pairs={{1,0},{2,1},{3,2},{5,4},{6,5},{7,6},{9,8},{10,9},{11,10},{13,12},{... | collective-permute-start | bytes 958472 | tf_op jit(solution)/shard_map/ppermute | solution.py:10
  24.8 58.1 %copy-start = (bf16[128,256]{1,0:T(8,128)(2,1)S(1)}, bf16[128,256]{1,0:T(8,128)(2,1)}, u32[]{:S(2)}) copy-start(bf16[128,256]{1,0:T(8,128)(2,1)} %param.9) | copy-start | bytes 196612
  24.8 89.1 %reduce-scatter.2.cloned.1.call-start = ((), (), s32[]{:S(2)}) async-start(), calls=%async_computation.2 | async-start | bytes 294912 | tf_op jit(solution)/shard_map/reduce_scatter | solution.py:36
Sparse Core Ops, SparseCore 0:
  24.9 53.8 all-gather.1
  83.0 30.8 reduce-scatter.1
where the time goes:
time: 121 us
  waiting for transfers between devices  81.4 us (67%)
  between operations  14.1 us (12%)
  matrix products  9.31 us (8%)
  blocking collectives  9 us (7%)
  other arithmetic  3.49 us (3%)
  local copies, waits for them, and re-layouts  2.12 us (2%)
  starting transfers between devices  1.36 us (1%)
    all_gather x1, waiting for transfers between devices, on_device(): whole = lax.all_gather(resampled, 'tm', axis=1, tiled=True)  54 us
    reduce_scatter x1, waiting for transfers between devices, on_device(): lax.psum_scatter(partial_value, 'space', scatter_dimension=0, tiled=True)  19.6 us
    all_gather x1, blocking collectives, on_device(): every_panel = lax.all_gather(panels, 'tm', axis=0, tiled=True)  9 us
    ppermute x1, waiting for transfers between devices, shifted(): lax.ppermute(value, axis, [(source, source + steps) for source in range(i...  7.78 us
    dot_general x1, matrix products, on_device(): lax.dot_general(resampled, whole, (((0,), (0,)), ((), ())), preferred_ele...  3.97 us
    dot_general x1, matrix products, on_device(): jnp.dot(extended, weights, preferred_element_type=jnp.float32)  2.9 us
    dot_general x1, matrix products, on_device(): jnp.dot(mine, every_panel, preferred_element_type=jnp.float32)  2.45 us
  transfers between devices with their start and end apart: 3, of which 3 were waited for; matrix products, arithmetic and copies ran while one was open for 5% of the time, Pallas kernels for 0%

commit v1 on v0

--- a/solution.py
+++ b/solution.py
@@ -25,7 +25,16 @@
     resampled = jnp.dot(extended, weights, preferred_element_type=jnp.float32).astype(jnp.bfloat16)
     scale = 1.0 / (rows * lax.axis_size("space"))
     share = rows // lax.axis_size("tm")
-    whole = lax.all_gather(resampled, "tm", axis=1, tiled=True)
+    u_next, val2 = (jax.lax.psum(1, "tm"), jax.lax.axis_index("tm"))
+    whole, near = (resampled, 1)
+    while near < u_next:
+        extra = jax.lax.ppermute(
+            whole, axis_name="tm", perm=[(jj, jj ^ near) for jj in range(u_next)]
+        )
+        t1 = jnp.concatenate([whole, extra], axis=1)
+        m_next = jnp.concatenate([extra, whole], 1)
+        whole = jnp.where(val2 & near == 0, t1, m_next)
+        near = 2 * near
     partial_value = lax.dot_general(
         resampled, whole, (((0,), (0,)), ((), ())), preferred_element_type=jnp.float32
     )

time: 121 us -> 143 us (1.18)
  waiting for transfers between devices: 81.4 us -> 95 us
  other arithmetic: 3.49 us -> 9.06 us
  starting transfers between devices: 1.36 us -> 4.95 us
  matrix products: 9.31 us -> 6.84 us
  local copies, waits for them, and re-layouts: 2.12 us -> 4.05 us
    ppermute x0 -> x2, waiting for transfers between devices: none -> 67.6 us  [on_device(): jax.lax.ppermute(whole, axis_name='tm', perm=[(jj, jj ^ near) for jj in r...]
    all_gather x1 -> x0, waiting for transfers between devices: 54 us -> none  [on_device(): whole = lax.all_gather(resampled, 'tm', axis=1, tiled=True)]
    select_n x0 -> x2, other arithmetic: none -> 5.57 us  [on_device(): whole = jnp.where(val2 & near == 0, t1, m_next)]
    ppermute x0 -> x2, starting transfers between devices: none -> 3.63 us  [on_device(): jax.lax.ppermute(whole, axis_name='tm', perm=[(jj, jj ^ near) for jj in r...]
    unnamed x3 -> x5, local copies, waits for them, and re-layouts: 1.63 us -> 3.55 us
    dot_general x1, matrix products: 3.97 us -> 2.28 us  [on_device(): lax.dot_general(resampled, whole, (((0,), (0,)), ((), ())), preferred_ele...]
  transfers between devices with their start and end apart: 3 -> 4, of which waited for: 3 -> 4; matrix products, arithmetic and copies ran while one was open for 5% -> 4% of each run, Pallas kernels for 0% -> 0%
where the time goes in v1:
time: 143 us
  waiting for transfers between devices  95 us (66%)
  between operations  14.1 us (10%)
  other arithmetic  9.06 us (6%)
  blocking collectives  8.93 us (6%)
  matrix products  6.84 us (5%)
  starting transfers between devices  4.95 us (3%)
  local copies, waits for them, and re-layouts  4.05 us (3%)
    ppermute x2, waiting for transfers between devices, on_device(): jax.lax.ppermute(whole, axis_name='tm', perm=[(jj, jj ^ near) for jj in r...  67.6 us
    reduce_scatter x1, waiting for transfers between devices, on_device(): lax.psum_scatter(partial_value, 'space', scatter_dimension=0, tiled=True)  19.6 us
    all_gather x1, blocking collectives, on_device(): every_panel = lax.all_gather(panels, 'tm', axis=0, tiled=True)  8.93 us
    ppermute x1, waiting for transfers between devices, shifted(): lax.ppermute(value, axis, [(source, source + steps) for source in range(i...  7.78 us
    select_n x2, other arithmetic, on_device(): whole = jnp.where(val2 & near == 0, t1, m_next)  5.57 us
    ppermute x2, starting transfers between devices, on_device(): jax.lax.ppermute(whole, axis_name='tm', perm=[(jj, jj ^ near) for jj in r...  3.63 us
    unnamed x5, local copies, waits for them, and re-layouts  3.55 us
  transfers between devices with their start and end apart: 4, of which 4 were waited for; matrix products, arithmetic and copies ran while one was open for 4% of the time, Pallas kernels for 0%

profile of v1, /device:TPU:0, one launch (start us, length us, event | category | flops | bytes accessed | tf_op | source)
XLA Modules:
  0.0 142.9 jit_solution(2327150253919211594)
XLA Ops:
  7.2 0.0 reduce-scatter.2.cloned.1.call-start
  7.2 1.6 %copy.11 = bf16[4096,39]{0,1:T(8,128)(2,1)S(1)} copy(bf16[4096,39]{1,0:T(8,128)(2,1)} %bitcast.7) | data formatting | bytes 638976
  8.8 1.3 collective-permute-start
  10.1 0.7 broadcast_subtract_fusion
  10.8 0.7 convert_bitcast_fusion
  11.5 0.7 iota_compare_fusion.1
  12.2 1.4 %select_reduce_fusion = bf16[167,128]{1,0:T(8,128)(2,1)S(1)} fusion(f32[40,128]{1,0:T(8,128)S(1)} %convert_bitcast_fusion, s32[167,128]{1,0:T(8,128)S(1)} %iota_subtract_fusion, pred[40,128]{1,0:T(8,128)(4,1)S(1)} %iota_compare_fusion.1), kind=kLoop, calls=%fused_computation.2 | loop fusion | flops 3398784 | bytes 153856 | tf_op jit(solution)/shard_map/reduce_sum | solution.py:24
  13.6 7.8 %collective-permute-done = bf16[4096,39]{0,1:T(8,128)(2,1)S(1)} collective-permute-done((bf16[4096,39]{0,1:T(8,128)(2,1)S(1)}, bf16[4096,39]{0,1:T(8,128)(2,1)S(1)}, u32[]{:S(2)}, u32[]{:S(2)}) %collective-permute-start) | collective-permute-done | bytes 319520 | tf_op jit(solution)/shard_map/ppermute | solution.py:10
  21.4 0.5 copy.10
  21.9 2.0 %convolution_convert_fusion = bf16[4096,128]{0,1:T(8,128)(2,1)S(1)} fusion(bf16[4096,39]{1,0:T(8,128)(2,1)S(1)} %copy.10, bf16[4096,128]{1,0:T(8,128)(2,1)} %param.5, bf16[167,128]{1,0:T(8,128)(2,1)S(1)} %select_reduce_fusion), kind=kOutput, calls=%fused_computation | convolution fusion | flops 178372608 | bytes 2459392 | tf_op jit(solution)/shard_map/dot_general | solution.py:25
  23.9 2.7 %collective-permute-start.1 = (bf16[4096,128]{0,1:T(8,128)(2,1)S(1)}, bf16[4096,128]{0,1:T(8,128)(2,1)}, u32[]{:S(2)}, u32[]{:S(2)}) collective-permute-start(bf16[4096,128]{0,1:T(8,128)(2,1)S(1)} %convolution_convert_fusion), channel_id=1, source_target_pairs={{0,1},{1,0},{2,3},{3,2},{4,5},{5,4},{6,7},{7,6},{8,9},{9,8},{10,11... | collective-permute-start | bytes 3145736 | tf_op jit(solution)/shard_map/ppermute | solution.py:31
  26.6 22.4 %collective-permute-done.1 = bf16[4096,128]{0,1:T(8,128)(2,1)} collective-permute-done((bf16[4096,128]{0,1:T(8,128)(2,1)S(1)}, bf16[4096,128]{0,1:T(8,128)(2,1)}, u32[]{:S(2)}, u32[]{:S(2)}) %collective-permute-start.1) | collective-permute-done | bytes 1048608 | tf_op jit(solution)/shard_map/ppermute | solution.py:31
  49.1 2.3 %maximum_select_fusion.1 = bf16[4096,256]{0,1:T(8,128)(2,1)S(1)} fusion(bf16[4096,128]{0,1:T(8,128)(2,1)} %collective-permute-done.1, bf16[4096,128]{0,1:T(8,128)(2,1)S(1)} %convolution_convert_fusion, pred[]{:T(512)S(6)} %eq.23), kind=kLoop, calls=%fused_computation.8 | loop fusion | flops 9437184 | bytes 4194305 | tf_op jit(solution)/shard_map/jit(_where)/select_n | solution.py:36
  51.3 0.9 collective-permute-start.2
  52.3 45.2 %collective-permute-done.2 = bf16[4096,256]{0,1:T(8,128)(2,1)} collective-permute-done((bf16[4096,256]{0,1:T(8,128)(2,1)S(1)}, bf16[4096,256]{0,1:T(8,128)(2,1)}, u32[]{:S(2)}, u32[]{:S(2)}) %collective-permute-start.2) | collective-permute-done | bytes 2097184 | tf_op jit(solution)/shard_map/ppermute | solution.py:31
  97.4 3.3 %maximum_select_fusion = bf16[4096,512]{0,1:T(8,128)(2,1)S(1)} fusion(bf16[4096,256]{0,1:T(8,128)(2,1)} %collective-permute-done.2, bf16[4096,256]{0,1:T(8,128)(2,1)S(1)} %maximum_select_fusion.1, pred[]{:T(512)S(6)} %eq.22), kind=kLoop, calls=%fused_computation.1 | loop fusion | flops 18874368 | bytes 8388609 | tf_op jit(solution)/shard_map/jit(_where)/select_n | solution.py:36
  100.7 0.0 copy-start
  100.8 1.9 %copy-done = bf16[4096,512]{0,1:T(8,128)(2,1)} copy-done((bf16[4096,512]{0,1:T(8,128)(2,1)}, bf16[4096,512]{0,1:T(8,128)(2,1)S(1)}, u32[]{:S(2)}) %copy-start) | copy-done | bytes 4194328
  102.7 2.3 %convolution_multiply_fusion = f32[128,512]{1,0:T(8,128)} fusion(bf16[4096,128]{0,1:T(8,128)(2,1)S(1)} %convolution_convert_fusion, bf16[4096,512]{0,1:T(8,128)(2,1)S(1)} %maximum_select_fusion), kind=kOutput, calls=%fused_computation.10 | convolution fusion | flops 536936448 | bytes 5505024 | tf_op jit(solution)/shard_map/dot_general | solution.py:38
  105.0 0.0 reduce-scatter.2.cloned.1.call-update
  105.0 0.0 copy-done.1
  105.0 8.9 %all_gather.3 = bf16[512,256]{1,0:T(8,128)(2,1)S(1)} all-gather(bf16[128,256]{1,0:T(8,128)(2,1)S(1)} %copy-done.1), channel_id=1, replica_groups=mesh['space'=8,'tm'=4] {'tm'}, dimensions={0}, use_global_device_ids=true | all-gather | bytes 327680 | tf_op jit(solution)/shard_map/all_gather | solution.py:41
  113.9 2.5 %convolution_convert_fusion.1 = bf16[1024,256]{1,0:T(8,128)(2,1)} fusion(bf16[512,256]{1,0:T(8,128)(2,1)S(1)} %all_gather.3, bf16[4096,512]{0,1:T(8,128)(2,1)} %copy-done, s32[]{:T(128)S(6)} %select_n.28), kind=kOutput, calls=%fused_computation.9 | convolution fusion | flops 268697600 | bytes 1835012 | tf_op jit(solution)/shard_map/dot_general | solution.py:43
  116.4 19.6 %reduce-scatter.2.cloned.1.call-done = f32[16,512]{1,0:T(8,128)} async-done(((f32[128,512]{1,0:T(8,128)}), f32[16,512]{1,0:T(8,128)}) %reduce-scatter.2.cloned.1.call-update) | async-done | bytes 32784 | tf_op jit(solution)/shard_map/reduce_scatter | solution.py:45
  (2 shorter events, 0.0 us)
Async XLA Ops:
  7.2 128.9 %reduce-scatter.2.cloned.1.call-start = ((), (), s32[]{:S(2)}) async-start(), calls=%async_computation.1 | async-start | bytes 294912 | tf_op jit(solution)/shard_map/reduce_scatter | solution.py:45
  8.8 12.6 %collective-permute-start = (bf16[4096,39]{0,1:T(8,128)(2,1)S(1)}, bf16[4096,39]{0,1:T(8,128)(2,1)S(1)}, u32[]{:S(2)}, u32[]{:S(2)}) collective-permute-start(bf16[4096,39]{0,1:T(8,128)(2,1)S(1)} %copy.11), channel_id=1, source_target_pairs={{1,0},{2,1},{3,2},{5,4},{6,5},{7,6},{9,8},{10,9},{11,10},{13,12},{... | collective-permute-start | bytes 958472 | tf_op jit(solution)/shard_map/ppermute | solution.py:10
  23.9 25.1 %collective-permute-start.1 = (bf16[4096,128]{0,1:T(8,128)(2,1)S(1)}, bf16[4096,128]{0,1:T(8,128)(2,1)}, u32[]{:S(2)}, u32[]{:S(2)}) collective-permute-start(bf16[4096,128]{0,1:T(8,128)(2,1)S(1)} %convolution_convert_fusion), channel_id=1, source_target_pairs={{0,1},{1,0},{2,3},{3,2},{4,5},{5,4},{6,7},{7,6},{8,9},{9,8},{10,11... | collective-permute-start | bytes 3145736 | tf_op jit(solution)/shard_map/ppermute | solution.py:31
  51.3 46.1 %collective-permute-start.2 = (bf16[4096,256]{0,1:T(8,128)(2,1)S(1)}, bf16[4096,256]{0,1:T(8,128)(2,1)}, u32[]{:S(2)}, u32[]{:S(2)}) collective-permute-start(bf16[4096,256]{0,1:T(8,128)(2,1)S(1)} %maximum_select_fusion.1), channel_id=1, source_target_pairs={{0,2},{1,3},{2,0},{3,1},{4,6},{5,7},{6,4},{7,5},{8,10},{9,11},{10,... | collective-permute-start | bytes 6291464 | tf_op jit(solution)/shard_map/ppermute | solution.py:31
  100.7 1.9 %copy-start = (bf16[4096,512]{0,1:T(8,128)(2,1)}, bf16[4096,512]{0,1:T(8,128)(2,1)S(1)}, u32[]{:S(2)}) copy-start(bf16[4096,512]{0,1:T(8,128)(2,1)S(1)} %maximum_select_fusion) | copy-start | bytes 12582916
  102.7 2.3 %copy-start.1 = (bf16[128,256]{1,0:T(8,128)(2,1)S(1)}, bf16[128,256]{1,0:T(8,128)(2,1)}, u32[]{:S(2)}) copy-start(bf16[128,256]{1,0:T(8,128)(2,1)} %param.9) | copy-start | bytes 196612
Sparse Core Ops, SparseCore 0:
  105.1 30.9 reduce-scatter.1
